TPU v7x, 32 devices: a whole 2x2x4 slice. The times are simulated.
32 devices in a mesh: group: 2 (over core), dp: 4 (over z), section: 2 (over x), tensor: 2 (over y).
Axes of the slice: x: 2, y: 2, z: 4, core: 2. Of those that a mesh axis runs over, the one named last changes fastest.
Arguments:
- merged: bfloat16 [768, 5120], P('dp'), may hold values from -6 to 6
- counts: int32 [8], P('dp'), may hold values from 4 to 384
- owners: int32 [768, 1], P('dp'), may hold values from 0 to 3; in each aligned block of 192 rows (0 to 191, 192 to 383, ...) at most 96 rows name the same one
- w_merge: bfloat16 [5120, 8192], P(None, ('group', 'section', 'tensor')), may hold values from -0.078125 to 0.078125
- norm_gain: float32 [8192], P(('group', 'section', 'tensor')), may hold values from 0.25 to 1.75
- cotangent: bfloat16 [4, 4, 96, 8192], P('dp', None, None, ('group', 'section', 'tensor')), may hold values from -6 to 6
Outputs:
- embedded: bfloat16 [4, 4, 96, 8192], P('dp', None, None, ('group', 'section', 'tensor'))
- grad_merged: float32 [768, 5120], P('dp', ('group', 'section', 'tensor'))
- grad_weight: float32 [5120, 8192], P('dp', ('group', 'section', 'tensor'))
Inputs may be any that keep to these rules, and one draw needn't show every extreme that they name: `owners`: in each replica's 192 rows no owner appears more than 96 times.
All inputs are finite; a program needn't handle non-finite values.
Results may differ from a plain program's by a relative error of at most 0.0049.
Values may be sent and summed in bfloat16 or wider, within the bound.
A program may use at most 64 MiB of HBM per device.

v0:
```python
import jax
import jax.numpy as jnp
from jax import lax
from jax.sharding import PartitionSpec as P

D = 8192


def on_device(merged, counts, owners, w_merge, norm_gain, cotangent):
    rows = merged.shape[0]
    columns = w_merge.shape[1]
    replicas = lax.axis_size("dp")
    slots = cotangent.shape[2]
    images = counts.shape[0]
    per_image = rows // images
    projected = jnp.dot(merged, w_merge, preferred_element_type=jnp.float32).astype(jnp.bfloat16)
    row_index = jnp.arange(rows, dtype=jnp.int32)
    image_of = row_index // per_image
    picked = image_of[:, None] == jnp.arange(images, dtype=jnp.int32)[None, :]
    count_of = jnp.sum(jnp.where(picked, counts[None, :], 0), axis=1)
    valid = (4 * (row_index % per_image) < count_of).astype(jnp.float32)
    masked = (projected.astype(jnp.float32) * valid[:, None]).astype(jnp.bfloat16)
    owner = owners[:, 0]
    hits = (owner[:, None] == jnp.arange(replicas, dtype=jnp.int32)[None, :]).astype(jnp.int32)
    before = jnp.cumsum(hits, axis=0) - hits
    slot_index = jnp.sum(before * hits, axis=1)
    target = owner * slots + slot_index
    placer = (jnp.arange(replicas * slots, dtype=jnp.int32)[:, None] == target[None, :]).astype(
        jnp.bfloat16
    )
    outgoing = jnp.dot(placer, masked, preferred_element_type=jnp.float32).astype(jnp.bfloat16)
    outgoing = outgoing.reshape(replicas, slots, columns)
    received = lax.all_to_all(outgoing, "dp", split_axis=0, concat_axis=0, tiled=True)
    values = received.astype(jnp.float32)
    square_sums = lax.psum(jnp.sum(values * values, axis=2), ("group", "section", "tensor"))
    scale = lax.rsqrt(square_sums / D + 1e-05)
    normed = (values * scale[:, :, None] * norm_gain[None, None, :]).astype(jnp.bfloat16)
    embedded = normed[None]
    grad_in = cotangent[0].astype(jnp.float32) * norm_gain[None, None, :]
    inner_sums = lax.psum(jnp.sum(grad_in * values, axis=2), ("group", "section", "tensor"))
    inner = inner_sums / D
    slot_grad = (scale[:, :, None] * grad_in - values * (scale**3 * inner)[:, :, None]).astype(
        jnp.bfloat16
    )
    returned = lax.all_to_all(slot_grad, "dp", split_axis=0, concat_axis=0, tiled=True)
    returned = returned.reshape(replicas * slots, columns)
    gathered = lax.dot_general(
        placer, returned, (((0,), (0,)), ((), ())), preferred_element_type=jnp.float32
    )
    back = (gathered * valid[:, None]).astype(jnp.bfloat16)
    input_terms = lax.dot_general(
        back, w_merge, (((1,), (1,)), ((), ())), preferred_element_type=jnp.float32
    )
    grad_merged = lax.psum_scatter(
        input_terms, ("group", "section", "tensor"), scatter_dimension=1, tiled=True
    )
    column_block = lax.all_to_all(merged, "dp", split_axis=1, concat_axis=0, tiled=True)
    grad_weight = lax.dot_general(
        column_block,
        lax.all_gather(back, "dp", axis=0, tiled=True),
        (((0,), (0,)), ((), ())),
        preferred_element_type=jnp.float32,
    )
    return (embedded, grad_merged, grad_weight)


def solution(mesh):
    placed = (
        P("dp", None),
        P("dp"),
        P("dp", None),
        P(None, ("group", "section", "tensor")),
        P(("group", "section", "tensor")),
        P("dp", None, None, ("group", "section", "tensor")),
    )
    return jax.shard_map(
        on_device,
        mesh=mesh,
        in_specs=placed,
        out_specs=(
            P("dp", None, None, ("group", "section", "tensor")),
            P("dp", ("group", "section", "tensor")),
            P("dp", ("group", "section", "tensor")),
        ),
        check_vma=False,
    )
```

profile of v0, /device:TPU:0, one launch (start us, length us, event | category | flops | bytes accessed | tf_op | source)
XLA Modules:
  0.0 182.4 jit_solution(6930971145670902794)
XLA Ops:
  8.0 0.0 all-gather.2.cloned.1.call-start
  8.1 0.7 iota_compare_fusion.3
  8.7 0.7 fusion.18
  9.5 1.2 reduce-window.6
  10.8 0.1 slice.12
  10.8 0.1 copy.23
  11.0 0.1 copy.24
  11.1 0.1 add_bitcast_fusion
  11.2 0.7 fusion.16
  11.9 0.7 multiply_add_fusion
  12.5 0.0 copy-start.2
  12.5 7.0 %convolution_convert_fusion = bf16[384,1024]{1,0:T(8,128)(2,1)S(1)} fusion(bf16[192,5120]{1,0:T(8,128)(2,1)} %param.6, bf16[5120,1024]{1,0:T(8,128)(2,1)} %param.9, f32[192]{0:T(256)S(1)} %compare_convert_fusion, s32[192]{0:T(256)S(1)} %multiply_add_fusion), kind=kOutput, calls=%fused_computation.14 | convolution fusion | flops 2165514240 | bytes 13239808 | tf_op jit(solution)/shard_map/dot_general | solution.py:31
  19.6 0.0 copy-start
  19.6 26.4 %all_to_all.29 = bf16[4,96,1024]{2,1,0:T(8,128)(2,1)S(1)} all-to-all(bf16[4,96,1024]{2,1,0:T(8,128)(2,1)S(1)} %bitcast.38), channel_id=1, replica_groups=mesh['group'=2,'dp'=4,'section'=2,'tensor'=2] {'dp'}, dimensions={0} | all-to-all | bytes 1572864 | tf_op jit(solution)/shard_map/all_to_all | solution.py:33
  46.0 0.0 copy-done.2
  46.0 0.0 copy-done
  46.0 0.4 fusion.3
  46.4 14.3 %all-reduce.1 = (f32[4,96]{1,0:T(4,128)S(1)}, f32[4,96]{1,0:T(4,128)S(1)}) all-reduce(f32[4,96]{1,0:T(4,128)S(1)} %get-tuple-element.19, f32[4,96]{1,0:T(4,128)S(1)} %get-tuple-element.18), channel_id=1, replica_groups=mesh['group'=2,'dp'=4,'section'=2,'tensor'=2] {'group','section','tensor'}, use_global_device_ids=true, to_apply=%region_5.6 | all-reduce | flops 768 | bytes 6144 | tf_op jit(solution)/shard_map/psum | solution.py:35
  60.7 1.4 fusion.5
  62.1 23.6 %all_to_all.30 = bf16[4,96,1024]{2,1,0:T(8,128)(2,1)S(1)} all-to-all(bf16[4,96,1024]{2,1,0:T(8,128)(2,1)S(1)} %get-tuple-element.22), channel_id=1, replica_groups=mesh['group'=2,'dp'=4,'section'=2,'tensor'=2] {'dp'}, dimensions={0} | all-to-all | bytes 1572864 | tf_op jit(solution)/shard_map/all_to_all | solution.py:45
  85.7 1.2 fusion.7
  86.9 0.0 all-gather.2.cloned.1.call-update
  86.9 0.0 reduce-scatter.2.cloned.1.call-start
  86.9 9.7 %fusion.21 = f32[192,5120]{1,0:T(8,128)} fusion(bf16[192,1024]{1,0:T(8,128)(2,1)} %fusion.7, bf16[5120,1024]{1,0:T(8,128)(2,1)} %param.9), kind=kOutput, calls=%fused_computation.48 | convolution fusion | flops 2013265920 | bytes 14811136 | tf_op jit(solution)/shard_map/dot_general | solution.py:51
  96.7 0.0 copy-start.1
  96.7 0.0 reduce-scatter.2.cloned.1.call-update
  96.7 1.5 copy-done.1
  98.2 0.1 copy.31
  98.3 64.7 %all_to_all.31 = bf16[192,4,1280]{2,0,1:T(8,128)(2,1)S(1)} all-to-all(bf16[192,4,1280]{2,0,1:T(8,128)(2,1)S(1)} %bitcast.34), channel_id=1, replica_groups=mesh['group'=2,'dp'=4,'section'=2,'tensor'=2] {'dp'}, dimensions={1} | all-to-all | bytes 3932160 | tf_op jit(solution)/shard_map/all_to_all | solution.py:57
  163.1 0.0 all-gather.2.cloned.1.call-done
  163.1 6.0 %convolution_bitcast_fusion = f32[1280,1024]{0,1:T(8,128)} fusion(bf16[768,1024]{1,0:T(8,128)(2,1)} %all-gather.2.cloned.1.call-done, bf16[768,1280]{1,0:T(8,128)(2,1)S(1)} %bitcast.37), kind=kOutput, calls=%fused_computation | convolution fusion | flops 2013265920 | bytes 8781824 | tf_op jit(solution)/shard_map/dot_general | solution.py:58
  169.1 5.9 %copy.26 = f32[1280,1024]{1,0:T(8,128)} copy(f32[1280,1024]{0,1:T(8,128)} %convolution_bitcast_fusion) | data formatting | bytes 10485760
  174.9 0.0 reduce-scatter.2.cloned.1.call-done
  (8 shorter events, 0.1 us)
Async XLA Ops:
  8.0 155.1 %all-gather.2.cloned.1.call-start = ((), (), s32[]{:S(2)}) async-start(), calls=%async_computation.5 | async-start | bytes 1966080 | tf_op jit(solution)/shard_map/all_gather | solution.py:60
  12.5 33.4 %copy-start.2 = (f32[1024]{0:T(1024)S(1)}, f32[1024]{0:T(1024)}, u32[]{:S(2)}) copy-start(f32[1024]{0:T(1024)} %param.10) | copy-start | bytes 12292
  19.6 26.4 %copy-start = (bf16[1,4,96,1024]{3,2,1,0:T(8,128)(2,1)S(1)}, bf16[1,4,96,1024]{3,2,1,0:T(8,128)(2,1)}, u32[]{:S(2)}) copy-start(bf16[1,4,96,1024]{3,2,1,0:T(8,128)(2,1)} %param.11) | copy-start | bytes 2359300
  86.9 88.1 %reduce-scatter.2.cloned.1.call-start = ((), (), s32[]{:S(2)}) async-start(), calls=%async_computation.4 | async-start | bytes 4423680 | tf_op jit(solution)/shard_map/reduce_scatter | solution.py:54
  96.7 1.5 copy-start.1
Sparse Core Ops, SparseCore 0:
  87.0 58.4 all-gather.1
Sparse Core Ops, SparseCore 1:
  96.8 46.7 reduce-scatter.1
where the time goes:
time: 183 us; the launch traced here: 182 us
  blocking collectives  129 us (70%)
  matrix products  23.9 us (13%)
  between operations  15.5 us (8%)
  local copies, waits for them, and re-layouts  7.84 us (4%)
  other arithmetic  6.04 us (3%)
    all_to_all x1, blocking collectives, on_device(): lax.all_to_all(merged, 'dp', split_axis=1, concat_axis=0, tiled=True)  64.7 us
    all_to_all x1, blocking collectives, on_device(): lax.all_to_all(outgoing, 'dp', split_axis=0, concat_axis=0, tiled=True)  26.4 us
    all_to_all x1, blocking collectives, on_device(): lax.all_to_all(slot_grad, 'dp', split_axis=0, concat_axis=0, tiled=True)  23.6 us
    psum x1, blocking collectives, on_device(): lax.psum(jnp.sum(values * values, axis=2), ('group', 'section', 'tensor'))  14.3 us
    dot_general x1, matrix products, on_device(): lax.dot_general(back, w_merge, (((1,), (1,)), ((), ())), preferred_elemen...  9.72 us
    unnamed x8, local copies, waits for them, and re-layouts  7.42 us
    dot_general x1, matrix products, on_device(): jnp.dot(placer, masked, preferred_element_type=jnp.float32)  7.02 us
    dot_general x1, matrix products, on_device(): lax.dot_general(column_block, lax.all_gather(back, 'dp', axis=0, tiled=Tr...  5.97 us
  transfers between devices with their start and end apart: 2, of which 0 were waited for; matrix products, arithmetic and copies ran while one was open for 12% of the time, Pallas kernels for 0%

commit v1 on v0

--- a/solution.py
+++ b/solution.py
@@ -4,6 +4,14 @@
 from jax.sharding import PartitionSpec as P
 
 D = 8192
+
+
+def fix_forms_all(local):
+    axis_id = "group"
+    axis_name = ("section", "tensor")
+    for h in (axis_name, axis_id):
+        local = jax.lax.psum(local, h)
+    return local
 
 
 def on_device(merged, counts, owners, w_merge, norm_gain, cotangent):
@@ -32,7 +40,7 @@
     outgoing = outgoing.reshape(replicas, slots, columns)
     received = lax.all_to_all(outgoing, "dp", split_axis=0, concat_axis=0, tiled=True)
     values = received.astype(jnp.float32)
-    square_sums = lax.psum(jnp.sum(values * values, axis=2), ("group", "section", "tensor"))
+    square_sums = fix_forms_all(jnp.sum(values * values, axis=2))
     scale = lax.rsqrt(square_sums / D + 1e-05)
     normed = (values * scale[:, :, None] * norm_gain[None, None, :]).astype(jnp.bfloat16)
     embedded = normed[None]

time: 183 us -> 195 us (1.066)
  blocking collectives: 129 us -> 142 us
    psum x1 -> x3, blocking collectives: 14.3 us -> 26.3 us  [the longest x1 14.3 us: on_device(): lax.psum(jnp.sum(grad_in * values, axis=2), ('group', 'section', 'tensor'))]
  transfers between devices with their start and end apart: 2 -> 2, of which waited for: 0 -> 0; matrix products, arithmetic and copies ran while one was open for 12% -> 11% of each run, Pallas kernels for 0% -> 0%
where the time goes in v1:
time: 195 us
  blocking collectives  142 us (73%)
  matrix products  23.8 us (12%)
  between operations  15.5 us (8%)
  local copies, waits for them, and re-layouts  7.84 us (4%)
  other arithmetic  6.04 us (3%)
    all_to_all x1, blocking collectives, on_device(): lax.all_to_all(merged, 'dp', split_axis=1, concat_axis=0, tiled=True)  65.8 us
    all_to_all x1, blocking collectives, on_device(): lax.all_to_all(outgoing, 'dp', split_axis=0, concat_axis=0, tiled=True)  26.4 us
    all_to_all x1, blocking collectives, on_device(): lax.all_to_all(slot_grad, 'dp', split_axis=0, concat_axis=0, tiled=True)  23.1 us
    psum x1, blocking collectives, on_device(): lax.psum(jnp.sum(grad_in * values, axis=2), ('group', 'section', 'tensor'))  14.3 us
    psum x2, blocking collectives, fix_forms_all(): local = jax.lax.psum(local, h)  12.1 us
    dot_general x1, matrix products, on_device(): lax.dot_general(back, w_merge, (((1,), (1,)), ((), ())), preferred_elemen...  9.66 us
    unnamed x8, local copies, waits for them, and re-layouts  7.42 us
    dot_general x1, matrix products, on_device(): jnp.dot(placer, masked, preferred_element_type=jnp.float32)  7.02 us
  transfers between devices with their start and end apart: 2, of which 0 were waited for; matrix products, arithmetic and copies ran while one was open for 11% of the time, Pallas kernels for 0%

profile of v1, /device:TPU:0, one launch (start us, length us, event | category | flops | bytes accessed | tf_op | source)
XLA Modules:
  0.0 194.9 jit_solution(7447554740939186800)
XLA Ops:
  8.0 0.0 all-gather.2.cloned.1.call-start
  8.1 0.7 iota_compare_fusion.3
  8.7 0.7 fusion.18
  9.5 1.2 reduce-window.6
  10.8 0.1 slice.12
  10.8 0.1 copy.23
  11.0 0.1 copy.24
  11.1 0.1 add_bitcast_fusion
  11.2 0.7 fusion.16
  11.9 0.7 multiply_add_fusion
  12.5 0.0 copy-start.2
  12.5 7.0 %convolution_convert_fusion = bf16[384,1024]{1,0:T(8,128)(2,1)S(1)} fusion(bf16[192,5120]{1,0:T(8,128)(2,1)} %param.6, bf16[5120,1024]{1,0:T(8,128)(2,1)} %param.9, f32[192]{0:T(256)S(1)} %compare_convert_fusion, s32[192]{0:T(256)S(1)} %multiply_add_fusion), kind=kOutput, calls=%fused_computation.14 | convolution fusion | flops 2165514240 | bytes 13239808 | tf_op jit(solution)/shard_map/dot_general | solution.py:39
  19.6 0.0 copy-start
  19.6 26.4 %all_to_all.29 = bf16[4,96,1024]{2,1,0:T(8,128)(2,1)S(1)} all-to-all(bf16[4,96,1024]{2,1,0:T(8,128)(2,1)S(1)} %bitcast.38), channel_id=1, replica_groups=mesh['group'=2,'dp'=4,'section'=2,'tensor'=2] {'dp'}, dimensions={0} | all-to-all | bytes 1572864 | tf_op jit(solution)/shard_map/all_to_all | solution.py:41
  46.0 0.0 copy-done.2
  46.0 0.0 copy-done
  46.0 0.4 fusion.3
  46.4 14.3 %psum.23 = f32[4,96]{1,0:T(4,128)S(1)} all-reduce(f32[4,96]{1,0:T(4,128)S(1)} %get-tuple-element.18), channel_id=1, replica_groups=mesh['group'=2,'dp'=4,'section'=2,'tensor'=2] {'group','section','tensor'}, use_global_device_ids=true, to_apply=%region_8.9 | all-reduce | flops 384 | bytes 3072 | tf_op jit(solution)/shard_map/psum | solution.py:48
  60.7 9.6 %psum.21 = f32[4,96]{1,0:T(4,128)S(1)} all-reduce(f32[4,96]{1,0:T(4,128)S(1)} %get-tuple-element.19), channel_id=1, replica_groups=mesh['group'=2,'dp'=4,'section'=2,'tensor'=2] {'section','tensor'}, use_global_device_ids=true, to_apply=%region_5.6 | all-reduce | flops 384 | bytes 3072 | tf_op jit(solution)/shard_map/psum | solution.py:13
  70.3 2.5 %psum.22 = f32[4,96]{1,0:T(4,128)S(1)} all-reduce(f32[4,96]{1,0:T(4,128)S(1)} %psum.21), channel_id=1, replica_groups=mesh['group'=2,'dp'=4,'section'=2,'tensor'=2] {'group'}, use_global_device_ids=true, to_apply=%region_6.7 | all-reduce | flops 384 | bytes 3072 | tf_op jit(solution)/shard_map/psum | solution.py:13
  72.8 1.4 fusion.5
  74.2 23.1 %all_to_all.30 = bf16[4,96,1024]{2,1,0:T(8,128)(2,1)S(1)} all-to-all(bf16[4,96,1024]{2,1,0:T(8,128)(2,1)S(1)} %get-tuple-element.20), channel_id=1, replica_groups=mesh['group'=2,'dp'=4,'section'=2,'tensor'=2] {'dp'}, dimensions={0} | all-to-all | bytes 1572864 | tf_op jit(solution)/shard_map/all_to_all | solution.py:53
  97.3 1.2 fusion.7
  98.5 0.0 all-gather.2.cloned.1.call-update
  98.5 0.0 reduce-scatter.2.cloned.1.call-start
  98.5 9.7 %fusion.21 = f32[192,5120]{1,0:T(8,128)} fusion(bf16[192,1024]{1,0:T(8,128)(2,1)} %fusion.7, bf16[5120,1024]{1,0:T(8,128)(2,1)} %param.9), kind=kOutput, calls=%fused_computation.48 | convolution fusion | flops 2013265920 | bytes 14811136 | tf_op jit(solution)/shard_map/dot_general | solution.py:59
  108.2 0.0 copy-start.1
  108.2 0.0 reduce-scatter.2.cloned.1.call-update
  108.2 1.5 copy-done.1
  109.7 0.1 copy.31
  109.9 65.8 %all_to_all.31 = bf16[192,4,1280]{2,0,1:T(8,128)(2,1)S(1)} all-to-all(bf16[192,4,1280]{2,0,1:T(8,128)(2,1)S(1)} %bitcast.34), channel_id=1, replica_groups=mesh['group'=2,'dp'=4,'section'=2,'tensor'=2] {'dp'}, dimensions={1} | all-to-all | bytes 3932160 | tf_op jit(solution)/shard_map/all_to_all | solution.py:65
  175.6 0.0 all-gather.2.cloned.1.call-done
  175.6 6.0 %convolution_bitcast_fusion = f32[1280,1024]{0,1:T(8,128)} fusion(bf16[768,1024]{1,0:T(8,128)(2,1)} %all-gather.2.cloned.1.call-done, bf16[768,1280]{1,0:T(8,128)(2,1)S(1)} %bitcast.37), kind=kOutput, calls=%fused_computation | convolution fusion | flops 2013265920 | bytes 8781824 | tf_op jit(solution)/shard_map/dot_general | solution.py:66
  181.6 5.9 %copy.26 = f32[1280,1024]{1,0:T(8,128)} copy(f32[1280,1024]{0,1:T(8,128)} %convolution_bitcast_fusion) | data formatting | bytes 10485760
  187.5 0.0 reduce-scatter.2.cloned.1.call-done
  (8 shorter events, 0.1 us)
Async XLA Ops:
  8.0 167.7 %all-gather.2.cloned.1.call-start = ((), (), s32[]{:S(2)}) async-start(), calls=%async_computation.5 | async-start | bytes 1966080 | tf_op jit(solution)/shard_map/all_gather | solution.py:68
  12.5 33.4 %copy-start.2 = (f32[1024]{0:T(1024)S(1)}, f32[1024]{0:T(1024)}, u32[]{:S(2)}) copy-start(f32[1024]{0:T(1024)} %param.10) | copy-start | bytes 12292
  19.6 26.4 %copy-start = (bf16[1,4,96,1024]{3,2,1,0:T(8,128)(2,1)S(1)}, bf16[1,4,96,1024]{3,2,1,0:T(8,128)(2,1)}, u32[]{:S(2)}) copy-start(bf16[1,4,96,1024]{3,2,1,0:T(8,128)(2,1)} %param.11) | copy-start | bytes 2359300
  98.5 89.0 %reduce-scatter.2.cloned.1.call-start = ((), (), s32[]{:S(2)}) async-start(), calls=%async_computation.4 | async-start | bytes 4423680 | tf_op jit(solution)/shard_map/reduce_scatter | solution.py:62
  108.2 1.5 copy-start.1
Sparse Core Ops, SparseCore 0:
  98.6 60.6 all-gather.1
Sparse Core Ops, SparseCore 1:
  108.3 47.7 reduce-scatter.1
